TPU v7x, 32 devices: a whole 2x2x4 slice. The times are simulated.
32 devices in a mesh: tm: 8 (over z, y), emit: 4 (over x, core).
Axes of the slice: x: 2, y: 2, z: 4, core: 2. Of those that a mesh axis runs over, the one named last changes fastest.
Arguments:
- observed: int32 [8, 512], P('emit', 'tm'), may hold values from 0 to 4095
- starts: int32 [8], P('emit'), may hold values from 0 to 255
- initial: float32 [256], replicated, may hold values from 0.1 to 1
- transition: float32 [256, 256], replicated, may hold values from 0 to 1, as said below
- emission: float32 [4096, 256], P('emit'), may hold values from 0.5 to 2
Outputs:
- posterior: float32 [8, 512, 256], P('emit', 'tm')
- new_emission: float32 [4096, 256], P(('tm', 'emit'))
- loglik: float32 [8], P('emit')
Inputs may be any that keep to these rules, and one draw needn't show every extreme that they name: `transition`: entries positive.
All inputs are finite; a program needn't handle non-finite values.
Results may differ from a plain program's by a relative error of at most 0.0003.
Values sent between devices are 32-bit elements; how exact they have to be, the bound alone decides.
No kernel may reach another device: no remote copies, remote signals or barrier semaphores. Data moves between devices by JAX's collectives and lax.ppermute only.
A program may use at most 128 MiB of HBM per device.

v0:
```python
import jax
import jax.numpy as jnp
from jax import lax
from jax.sharding import PartitionSpec as P

highest = lax.Precision.HIGHEST
pseudo_count = 0.01


def from_behind(value, axis, by):
    peers = lax.axis_size(axis)
    pairs = [(i, i + by) for i in range(peers) if 0 <= i + by < peers]
    return lax.ppermute(value, axis, pairs)


def normalize_rows(values):
    return values / jnp.sum(values, axis=-1, keepdims=True)


def normalize_blocks(matrices):
    return matrices / jnp.sum(matrices, axis=(1, 2), keepdims=True)


def shards(observed, starts, initial, transition, emission):
    traj_rows, frame_count = observed.shape
    states = transition.shape[0]
    tm_count = lax.axis_size("tm")
    tm_place = lax.axis_index("tm")
    emit_count = lax.axis_size("emit")
    own_rows = emission.shape[0]
    total_rows = own_rows * emit_count
    positions = tm_place * frame_count + jnp.arange(frame_count, dtype=jnp.int32)
    active = positions[None, :] >= starts[:, None]
    block_rows = lax.all_gather(emission, "emit", axis=0, tiled=True)
    local_ids = observed
    inside = (local_ids >= 0) & (local_ids < block_rows.shape[0])
    taken = jnp.take(block_rows, jnp.clip(local_ids, 0, block_rows.shape[0] - 1), axis=0)
    weights = jnp.where(inside[:, :, None], taken, 0.0)
    weight_seq = jnp.swapaxes(weights, 0, 1)
    active_seq = active.T
    eye_block = jnp.broadcast_to(jnp.eye(states, dtype=jnp.float32), (traj_rows, states, states))

    def product_step(carried, inputs):
        weight_now, active_now = inputs
        moved = (
            jnp.einsum("nij,jk->nik", carried, transition, precision=highest)
            * weight_now[:, None, :]
        )
        moved = normalize_blocks(moved)
        return (jnp.where(active_now[:, None, None], moved, carried), None)

    transfer, _ = lax.scan(product_step, eye_block, (weight_seq, active_seq))
    prior_state = jnp.broadcast_to(initial / jnp.sum(initial), (traj_rows, states))
    final_state = jnp.full((traj_rows, states), 1.0 / states, jnp.float32)

    def relay_round(round_index, carried):
        forward_in, backward_in = carried
        forward_out = normalize_rows(
            jnp.einsum("ni,nij->nj", forward_in, transfer, precision=highest)
        )
        backward_out = normalize_rows(
            jnp.einsum("nij,nj->ni", transfer, backward_in, precision=highest)
        )
        from_left = from_behind(forward_out, "tm", 1)
        from_right = from_behind(backward_out, "tm", -1)
        forward_in = jnp.where(tm_place == 0, prior_state, from_left)
        backward_in = jnp.where(tm_place == tm_count - 1, final_state, from_right)
        return (forward_in, backward_in)

    forward_in, backward_in = lax.fori_loop(
        0, tm_count - 1, relay_round, (prior_state, final_state)
    )

    def forward_step(previous, inputs):
        weight_now, active_now = inputs
        moved = jnp.dot(previous, transition, precision=highest) * weight_now
        scaling = jnp.sum(moved, axis=1)
        updated = jnp.where(active_now[:, None], moved / scaling[:, None], previous)
        return (updated, (updated, jnp.where(active_now, jnp.log(scaling), 0.0)))

    _, (forward, log_scales) = lax.scan(forward_step, forward_in, (weight_seq, active_seq))

    def backward_step(later_msg, inputs):
        weight_now, active_now = inputs
        moved = jnp.dot(later_msg * weight_now, transition.T, precision=highest)
        earlier = jnp.where(active_now[:, None], normalize_rows(moved), later_msg)
        return (earlier, later_msg)

    _, backward = lax.scan(backward_step, backward_in, (weight_seq, active_seq), reverse=True)
    joint_prob = forward * backward
    occupancy = jnp.where(active_seq[:, :, None], normalize_rows(joint_prob), 0.0)
    posterior = jnp.swapaxes(states * occupancy, 0, 1)
    loglik_local = jnp.sum(log_scales, axis=0)
    occ_rows = jnp.swapaxes(occupancy, 0, 1).reshape(-1, states)
    frame_list = observed.reshape(-1)
    block = total_rows // (tm_count * emit_count)
    local_ids = frame_list
    inside = (local_ids >= 0) & (local_ids < block * lax.axis_size(("tm", "emit")))
    counts = lax.psum_scatter(
        jax.ops.segment_sum(
            jnp.where(inside[:, None], occ_rows, 0.0),
            jnp.clip(local_ids, 0, block * lax.axis_size(("tm", "emit")) - 1),
            num_segments=block * lax.axis_size(("tm", "emit")),
        ),
        ("tm", "emit"),
        scatter_dimension=0,
        tiled=True,
    )
    totals = lax.psum(jnp.sum(counts, axis=0), ("tm", "emit"))
    loglik_sum = lax.psum(loglik_local, "tm")
    new_emission = total_rows * (counts + pseudo_count) / (totals + total_rows * pseudo_count)
    loglik = loglik_sum / (frame_count * tm_count - starts).astype(jnp.float32)
    return (posterior, new_emission, loglik)


def solution(mesh):
    in_specs = (P("emit", "tm"), P("emit"), P(), P(), P("emit", None))
    out_specs = (P("emit", "tm", None), P(("tm", "emit"), None), P("emit"))
    return jax.shard_map(shards, mesh=mesh, in_specs=in_specs, out_specs=out_specs, check_vma=False)
```

profile of v0, /device:TPU:10, one launch (start us, length us, event | category | flops | bytes accessed | tf_op | source)
XLA Modules:
  0.0 506.8 jit_solution(13056474050517089215)
XLA Ops:
  13.1 31.2 %all-gather.2.cloned.1.call-done = f32[4096,256]{1,0:T(8,128)} async-done(((f32[1024,256]{1,0:T(8,128)}), f32[4096,256]{1,0:T(8,128)}) %all-gather.2.cloned.1.call-update) | async-done | bytes 4194320 | tf_op jit(solution)/shard_map/all_gather | solution.py:34
  44.2 2.9 gather_fusion
  47.4 117.4 %while.55 = (s32[]{:T(128)}, f32[2,256,256]{2,1,0:T(8,128)S(1)}, pred[64,2]{1,0:T(8,128)(4,1)S(1)}, f32[256,256]{1,0:T(8,128)}, f32[64,2,256]{2,1,0:T(2,128)S(1)}, /*index=5*/s32[]{:T(128)}) while((s32[]{:T(128)}, f32[2,256,256]{2,1,0:T(8,128)S(1)}, pred[64,2]{1,0:T(8,128)(4,1)S(1)}, f32[256,256]{1,0:T(8,128)}, f32[64,2,256]{2,1,0:T(2,128)S(1)}, ...), condition=%wide.region_3.4_spmd, body=%wide.region_1.3_spmd.sunk | while | flops 403177472 | bytes 2889835 | solution.py:52
  164.9 68.8 %while.58 = (s32[]{:T(128)}, f32[2,256]{1,0:T(2,128)S(1)}, f32[2,256]{1,0:T(2,128)S(1)}, pred[]{:T(512)}, f32[2,256,256]{2,1,0:T(8,128)S(1)}, /*index=5*/pred[]{:T(512)}, f32[256]{0:T(256)S(1)}, s32[]{:T(128)}, s32[]{:T(128)}) while((s32[]{:T(128)}, f32[2,256]{1,0:T(2,128)S(1)}, f32[2,256]{1,0:T(2,128)S(1)}, pred[]{:T(512)}, ...), condition=%wide.region_7.8_spmd.clone, body=%wide.region_4.7_spmd.clone.sunk | while | flops 3149311 | bytes 1098969 | solution.py:70
  165.6 3.4 collective-permute-start.1
  169.6 2.5 collective-permute-start
  172.1 3.9 collective-permute-done
  179.2 3.9 collective-permute-start
  183.1 2.4 collective-permute-done
  188.8 3.9 collective-permute-start
  192.7 2.4 collective-permute-done
  198.4 3.9 collective-permute-start
  202.4 2.4 collective-permute-done
  208.0 3.9 collective-permute-start
  212.0 2.4 collective-permute-done
  217.6 3.9 collective-permute-start
  221.6 2.4 collective-permute-done
  227.3 3.9 collective-permute-start
  233.7 38.5 %while.57 = (s32[]{:T(128)}, f32[2,256]{1,0:T(2,128)S(1)}, f32[64,2,256]{2,0,1:T(8,128)S(1)}, pred[64,2]{1,0:T(8,128)(4,1)S(1)}, f32[64,2,256]{2,1,0:T(2,128)S(1...) while((s32[]{:T(128)}, f32[2,256]{1,0:T(2,128)S(1)}, f32[64,2,256]{2,0,1:T(8,128)S(1)}, ...), condition=%wide.region_13.14_spmd, body=%wide.region_11.13_spmd.sunk | while | flops 1574913 | bytes 282763 | solution.py:89
  272.2 36.6 %while.56 = (s32[]{:T(128)}, f32[2,256]{1,0:T(2,128)S(1)}, f32[64,2,256]{2,0,1:T(8,128)S(1)}, f32[64,2]{1,0:T(8,128)S(1)}, pred[64,2]{1,0:T(8,128)(4,1)S(1)}, /*...) while((s32[]{:T(128)}, f32[2,256]{1,0:T(2,128)S(1)}, ...), condition=%wide.region_10.11_spmd, body=%wide.region_8.10_spmd.sunk | while | flops 1574914 | bytes 282801 | solution.py:81
  309.3 3.4 scatter_custom_fusion
  312.7 20.5 %psum.15 = f32[2]{0:T(128)S(1)} all-reduce(f32[2]{0:T(128)S(1)} %reduce_sum.94), channel_id=1, replica_groups=mesh['tm'=8,'emit'=4] {'tm'}, use_global_device_ids=true, to_apply=%region_20.21 | all-reduce | flops 2 | bytes 16 | tf_op jit(solution)/shard_map/psum | solution.py:110
  334.4 99.9 %reduce-scatter.2.cloned.1.call-done = f32[128,256]{1,0:T(8,128)} async-done(((f32[4096,256]{1,0:T(8,128)}), f32[128,256]{1,0:T(8,128)}) %reduce-scatter.2.cloned.1.call-update) | async-done | bytes 131088 | tf_op jit(solution)/shard_map/reduce_scatter | solution.py:99
  435.3 63.1 %psum.14 = f32[256]{0:T(256)S(1)} all-reduce(f32[256]{0:T(256)S(1)} %reduce_sum.93), channel_id=1, replica_groups=mesh['tm'=8,'emit'=4] {'tm','emit'}, use_global_device_ids=true, to_apply=%region_18.19 | all-reduce | flops 256 | bytes 2048 | tf_op jit(solution)/shard_map/psum | solution.py:109
  (1137 shorter events, 217.7 us)
Async XLA Ops:
  7.2 37.1 %all-gather.2.cloned.1.call-start = ((), (), s32[]{:S(2)}) async-start(), calls=%async_computation.1 | async-start | bytes 5242880 | tf_op jit(solution)/shard_map/all_gather | solution.py:34
  7.9 426.4 %reduce-scatter.2.cloned.1.call-start = ((), (), s32[]{:S(2)}) async-start(), calls=%async_computation.2 | async-start | bytes 4325376 | tf_op jit(solution)/shard_map/reduce_scatter | solution.py:99
  164.8 68.8 %copy-start = (f32[256,256]{1,0:T(8,128)S(1)}, f32[256,256]{1,0:T(8,128)}, u32[]{:S(2)}) copy-start(f32[256,256]{1,0:T(8,128)} %get-tuple-element.664) | copy-start | bytes 786436
  165.6 6.4 %collective-permute-start.1 = (f32[2,256]{1,0:T(2,128)S(1)}, f32[2,256]{1,0:T(2,128)S(1)}, u32[]{:S(2)}, u32[]{:S(2)}) collective-permute-start(f32[2,256]{1,0:T(2,128)S(1)} %bitcast_divide_fusion.5), channel_id=1, source_target_pairs={{4,0},{8,4},{12,8},{16,12},{20,16},{24,20},{28,24},{5,1},{9,5},{13... | collective-permute-start | bytes 6152 | tf_op jit(solution)/shard_map/while/body/eval_jaxpr/ppermute | solution.py:13
  169.6 6.4 %collective-permute-start = (f32[2,256]{1,0:T(2,128)S(1)}, f32[2,256]{1,0:T(2,128)S(1)}, u32[]{:S(2)}, u32[]{:S(2)}) collective-permute-start(f32[2,256]{1,0:T(2,128)S(1)} %bitcast_divide_fusion.4), channel_id=1, source_target_pairs={{0,4},{4,8},{8,12},{12,16},{16,20},{20,24},{24,28},{1,5},{5,9},{9,... | collective-permute-start | bytes 6152 | tf_op jit(solution)/shard_map/while/body/eval_jaxpr/ppermute | solution.py:13
  176.7 6.4 %collective-permute-start.1 = (f32[2,256]{1,0:T(2,128)S(1)}, f32[2,256]{1,0:T(2,128)S(1)}, u32[]{:S(2)}, u32[]{:S(2)}) collective-permute-start(f32[2,256]{1,0:T(2,128)S(1)} %bitcast_divide_fusion.5), channel_id=1, source_target_pairs={{4,0},{8,4},{12,8},{16,12},{20,16},{24,20},{28,24},{5,1},{9,5},{13... | collective-permute-start | bytes 6152 | tf_op jit(solution)/shard_map/while/body/eval_jaxpr/ppermute | solution.py:13
  179.2 6.4 %collective-permute-start = (f32[2,256]{1,0:T(2,128)S(1)}, f32[2,256]{1,0:T(2,128)S(1)}, u32[]{:S(2)}, u32[]{:S(2)}) collective-permute-start(f32[2,256]{1,0:T(2,128)S(1)} %bitcast_divide_fusion.4), channel_id=1, source_target_pairs={{0,4},{4,8},{8,12},{12,16},{16,20},{20,24},{24,28},{1,5},{5,9},{9,... | collective-permute-start | bytes 6152 | tf_op jit(solution)/shard_map/while/body/eval_jaxpr/ppermute | solution.py:13
  186.3 6.4 %collective-permute-start.1 = (f32[2,256]{1,0:T(2,128)S(1)}, f32[2,256]{1,0:T(2,128)S(1)}, u32[]{:S(2)}, u32[]{:S(2)}) collective-permute-start(f32[2,256]{1,0:T(2,128)S(1)} %bitcast_divide_fusion.5), channel_id=1, source_target_pairs={{4,0},{8,4},{12,8},{16,12},{20,16},{24,20},{28,24},{5,1},{9,5},{13... | collective-permute-start | bytes 6152 | tf_op jit(solution)/shard_map/while/body/eval_jaxpr/ppermute | solution.py:13
  188.8 6.4 %collective-permute-start = (f32[2,256]{1,0:T(2,128)S(1)}, f32[2,256]{1,0:T(2,128)S(1)}, u32[]{:S(2)}, u32[]{:S(2)}) collective-permute-start(f32[2,256]{1,0:T(2,128)S(1)} %bitcast_divide_fusion.4), channel_id=1, source_target_pairs={{0,4},{4,8},{8,12},{12,16},{16,20},{20,24},{24,28},{1,5},{5,9},{9,... | collective-permute-start | bytes 6152 | tf_op jit(solution)/shard_map/while/body/eval_jaxpr/ppermute | solution.py:13
  195.9 6.4 %collective-permute-start.1 = (f32[2,256]{1,0:T(2,128)S(1)}, f32[2,256]{1,0:T(2,128)S(1)}, u32[]{:S(2)}, u32[]{:S(2)}) collective-permute-start(f32[2,256]{1,0:T(2,128)S(1)} %bitcast_divide_fusion.5), channel_id=1, source_target_pairs={{4,0},{8,4},{12,8},{16,12},{20,16},{24,20},{28,24},{5,1},{9,5},{13... | collective-permute-start | bytes 6152 | tf_op jit(solution)/shard_map/while/body/eval_jaxpr/ppermute | solution.py:13
  198.4 6.4 %collective-permute-start = (f32[2,256]{1,0:T(2,128)S(1)}, f32[2,256]{1,0:T(2,128)S(1)}, u32[]{:S(2)}, u32[]{:S(2)}) collective-permute-start(f32[2,256]{1,0:T(2,128)S(1)} %bitcast_divide_fusion.4), channel_id=1, source_target_pairs={{0,4},{4,8},{8,12},{12,16},{16,20},{20,24},{24,28},{1,5},{5,9},{9,... | collective-permute-start | bytes 6152 | tf_op jit(solution)/shard_map/while/body/eval_jaxpr/ppermute | solution.py:13
  205.5 6.4 %collective-permute-start.1 = (f32[2,256]{1,0:T(2,128)S(1)}, f32[2,256]{1,0:T(2,128)S(1)}, u32[]{:S(2)}, u32[]{:S(2)}) collective-permute-start(f32[2,256]{1,0:T(2,128)S(1)} %bitcast_divide_fusion.5), channel_id=1, source_target_pairs={{4,0},{8,4},{12,8},{16,12},{20,16},{24,20},{28,24},{5,1},{9,5},{13... | collective-permute-start | bytes 6152 | tf_op jit(solution)/shard_map/while/body/eval_jaxpr/ppermute | solution.py:13
  208.0 6.4 %collective-permute-start = (f32[2,256]{1,0:T(2,128)S(1)}, f32[2,256]{1,0:T(2,128)S(1)}, u32[]{:S(2)}, u32[]{:S(2)}) collective-permute-start(f32[2,256]{1,0:T(2,128)S(1)} %bitcast_divide_fusion.4), channel_id=1, source_target_pairs={{0,4},{4,8},{8,12},{12,16},{16,20},{20,24},{24,28},{1,5},{5,9},{9,... | collective-permute-start | bytes 6152 | tf_op jit(solution)/shard_map/while/body/eval_jaxpr/ppermute | solution.py:13
  215.2 6.4 %collective-permute-start.1 = (f32[2,256]{1,0:T(2,128)S(1)}, f32[2,256]{1,0:T(2,128)S(1)}, u32[]{:S(2)}, u32[]{:S(2)}) collective-permute-start(f32[2,256]{1,0:T(2,128)S(1)} %bitcast_divide_fusion.5), channel_id=1, source_target_pairs={{4,0},{8,4},{12,8},{16,12},{20,16},{24,20},{28,24},{5,1},{9,5},{13... | collective-permute-start | bytes 6152 | tf_op jit(solution)/shard_map/while/body/eval_jaxpr/ppermute | solution.py:13
  217.6 6.4 %collective-permute-start = (f32[2,256]{1,0:T(2,128)S(1)}, f32[2,256]{1,0:T(2,128)S(1)}, u32[]{:S(2)}, u32[]{:S(2)}) collective-permute-start(f32[2,256]{1,0:T(2,128)S(1)} %bitcast_divide_fusion.4), channel_id=1, source_target_pairs={{0,4},{4,8},{8,12},{12,16},{16,20},{20,24},{24,28},{1,5},{5,9},{9,... | collective-permute-start | bytes 6152 | tf_op jit(solution)/shard_map/while/body/eval_jaxpr/ppermute | solution.py:13
  224.8 6.4 %collective-permute-start.1 = (f32[2,256]{1,0:T(2,128)S(1)}, f32[2,256]{1,0:T(2,128)S(1)}, u32[]{:S(2)}, u32[]{:S(2)}) collective-permute-start(f32[2,256]{1,0:T(2,128)S(1)} %bitcast_divide_fusion.5), channel_id=1, source_target_pairs={{4,0},{8,4},{12,8},{16,12},{20,16},{24,20},{28,24},{5,1},{9,5},{13... | collective-permute-start | bytes 6152 | tf_op jit(solution)/shard_map/while/body/eval_jaxpr/ppermute | solution.py:13
  227.3 6.4 %collective-permute-start = (f32[2,256]{1,0:T(2,128)S(1)}, f32[2,256]{1,0:T(2,128)S(1)}, u32[]{:S(2)}, u32[]{:S(2)}) collective-permute-start(f32[2,256]{1,0:T(2,128)S(1)} %bitcast_divide_fusion.4), channel_id=1, source_target_pairs={{0,4},{4,8},{8,12},{12,16},{16,20},{20,24},{24,28},{1,5},{5,9},{9,... | collective-permute-start | bytes 6152 | tf_op jit(solution)/shard_map/while/body/eval_jaxpr/ppermute | solution.py:13
  309.3 24.0 %copy-start.1 = (s32[2]{0:T(128)S(1)}, s32[2]{0:T(128)}, u32[]{:S(2)}) copy-start(s32[2]{0:T(128)} %param.14) | copy-start | bytes 28
Sparse Core Ops, SparseCore 0:
  9.5 34.6 all-gather.1
  312.8 121.4 reduce-scatter.1
where the time goes:
time: 510 us; the launch traced here: 507 us
  matrix products  159 us (31%)
  waiting for transfers between devices  150 us (29%)
  blocking collectives  83.6 us (16%)
  starting transfers between devices  41 us (8%)
  other arithmetic  36.2 us (7%)
  local copies, waits for them, and re-layouts  14.3 us (3%)
  between operations  14.2 us (3%)
  loops' own time  8.47 us (2%)
    dot_general x64, matrix products, product_step(): jnp.einsum('nij,jk->nik', carried, transition, precision=highest)  104 us
    reduce_scatter x1, waiting for transfers between devices, shards(): lax.psum_scatter(jax.ops.segment_sum(jnp.where(inside[:, None], occ_rows,...  99.9 us
    psum x1, blocking collectives, shards(): totals = lax.psum(jnp.sum(counts, axis=0), ('tm', 'emit'))  63.1 us
    ppermute x14, starting transfers between devices, from_behind(): return lax.ppermute(value, axis, pairs)  40.9 us
    all_gather x1, waiting for transfers between devices, shards(): block_rows = lax.all_gather(emission, 'emit', axis=0, tiled=True)  31.2 us
    dot_general x64, matrix products, backward_step(): moved = jnp.dot(later_msg * weight_now, transition.T, precision=highest)  27.4 us
    dot_general x64, matrix products, forward_step(): moved = jnp.dot(previous, transition, precision=highest) * weight_now  21.3 us
    psum x1, blocking collectives, shards(): loglik_sum = lax.psum(loglik_local, 'tm')  20.5 us
  transfers between devices with their start and end apart: 16, of which 9 were waited for; matrix products, arithmetic and copies ran while one was open for 2% of the time, Pallas kernels for 0%

commit v1 on v0

--- a/solution.py
+++ b/solution.py
@@ -5,6 +5,14 @@
 
 highest = lax.Precision.HIGHEST
 pseudo_count = 0.01
+
+
+def tiled_gather(shard, axis, dim):
+    length = lax.axis_size(axis)
+    repeats = [length if d == dim else 1 for d in range(shard.ndim)]
+    return lax.all_to_all(
+        jnp.tile(shard, repeats), axis, split_axis=dim, concat_axis=dim, tiled=True
+    )
 
 
 def from_behind(value, axis, by):
@@ -31,7 +39,7 @@
     total_rows = own_rows * emit_count
     positions = tm_place * frame_count + jnp.arange(frame_count, dtype=jnp.int32)
     active = positions[None, :] >= starts[:, None]
-    block_rows = lax.all_gather(emission, "emit", axis=0, tiled=True)
+    block_rows = tiled_gather(emission, "emit", 0)
     local_ids = observed
     inside = (local_ids >= 0) & (local_ids < block_rows.shape[0])
     taken = jnp.take(block_rows, jnp.clip(local_ids, 0, block_rows.shape[0] - 1), axis=0)

time: 510 us -> 463 us (0.908)
  matrix products: 159 us -> 97.8 us
  waiting for transfers between devices: 150 us -> 163 us
  starting transfers between devices: 41 us -> 46.4 us
    dot_general x64, matrix products: 104 us -> 42.9 us  [product_step(): jnp.einsum('nij,jk->nik', carried, transition, precision=highest)]
    all_to_all x0 -> x1, waiting for transfers between devices: none -> 44.9 us  [tiled_gather(): lax.all_to_all(jnp.tile(shard, repeats), axis, split_axis=dim, concat_axi...]
    all_gather x1 -> x0, waiting for transfers between devices: 31.2 us -> none  [shards(): block_rows = lax.all_gather(emission, 'emit', axis=0, tiled=True)]
    all_to_all x0 -> x1, starting transfers between devices: none -> 5.49 us  [tiled_gather(): lax.all_to_all(jnp.tile(shard, repeats), axis, split_axis=dim, concat_axi...]
  transfers between devices with their start and end apart: 16 -> 16, of which waited for: 9 -> 9; matrix products, arithmetic and copies ran while one was open for 2% -> 1% of each run, Pallas kernels for 0% -> 0%
where the time goes in v1:
time: 463 us; the launch traced here: 462 us
  waiting for transfers between devices  163 us (35%)
  matrix products  97.8 us (21%)
  blocking collectives  83.8 us (18%)
  starting transfers between devices  46.4 us (10%)
  other arithmetic  32.9 us (7%)
  local copies, waits for them, and re-layouts  16.4 us (4%)
  between operations  14.2 us (3%)
  loops' own time  7.3 us (2%)
    reduce_scatter x1, waiting for transfers between devices, shards(): lax.psum_scatter(jax.ops.segment_sum(jnp.where(inside[:, None], occ_rows,...  100 us
    psum x1, blocking collectives, shards(): totals = lax.psum(jnp.sum(counts, axis=0), ('tm', 'emit'))  63.3 us
    all_to_all x1, waiting for transfers between devices, tiled_gather(): lax.all_to_all(jnp.tile(shard, repeats), axis, split_axis=dim, concat_axi...  44.9 us
    dot_general x64, matrix products, product_step(): jnp.einsum('nij,jk->nik', carried, transition, precision=highest)  42.9 us
    ppermute x14, starting transfers between devices, from_behind(): return lax.ppermute(value, axis, pairs)  40.9 us
    dot_general x64, matrix products, backward_step(): moved = jnp.dot(later_msg * weight_now, transition.T, precision=highest)  27.2 us
    dot_general x64, matrix products, forward_step(): moved = jnp.dot(previous, transition, precision=highest) * weight_now  21.3 us
    psum x1, blocking collectives, shards(): loglik_sum = lax.psum(loglik_local, 'tm')  20.5 us
  transfers between devices with their start and end apart: 16, of which 9 were waited for; matrix products, arithmetic and copies ran while one was open for 1% of the time, Pallas kernels for 0%

profile of v1, /device:TPU:10, one launch (start us, length us, event | category | flops | bytes accessed | tf_op | source)
XLA Modules:
  0.0 462.3 jit_solution(18053498641823166624)
XLA Ops:
  7.2 3.5 tile.2
  10.7 5.5 %all-to-all-start = ((f32[4,1024,256]{2,1,0:T(8,128)}), f32[4,1024,256]{2,1,0:T(8,128)}, u32[]{:S(2)}, u32[]{:S(2)}) async-start(f32[4,1024,256]{2,1,0:T(8,128)} %tile.2), calls=%async_computation | async-start | bytes 8388608 | tf_op jit(solution)/shard_map/all_to_all | solution.py:13
  18.0 44.9 %all-to-all-done = f32[4,1024,256]{2,1,0:T(8,128)} async-done(((f32[4,1024,256]{2,1,0:T(8,128)}), f32[4,1024,256]{2,1,0:T(8,128)}, u32[]{:S(2)}, u32[]{:S(2)}) %all-to-all-start) | async-done | bytes 4194336 | tf_op jit(solution)/shard_map/all_to_all | solution.py:13
  62.8 2.9 gather_fusion
  66.0 55.8 %while.55 = (s32[]{:T(128)}, f32[2,256,256]{2,1,0:T(8,128)S(1)}, pred[64,2]{1,0:T(8,128)(4,1)S(1)}, f32[256,256]{1,0:T(8,128)S(1)}, f32[64,2,256]{2,1,0:T(2,128)S(1)}, /*index=5*/s32[]{:T(128)}) while((s32[]{:T(128)}, f32[2,256,256]{2,1,0:T(8,128)S(1)}, pred[64,2]{1,0:T(8,128)(4,1)S(1)}, f32[256,256]{1,0:T(8,128)S(1)}, ...), condition=%wide.region_3.4_spmd, body=%wide.region_1.3_spmd.sunk | while | flops 403177472 | bytes 2889827 | solution.py:60
  121.8 68.7 %while.58 = (s32[]{:T(128)}, f32[2,256]{1,0:T(2,128)S(1)}, f32[2,256]{1,0:T(2,128)S(1)}, pred[]{:T(512)}, f32[2,256,256]{2,1,0:T(8,128)S(1)}, /*index=5*/pred[]{:T(512)}, f32[256]{0:T(256)S(1)}, s32[]{:T(128)}, s32[]{:T(128)}) while((s32[]{:T(128)}, f32[2,256]{1,0:T(2,128)S(1)}, f32[2,256]{1,0:T(2,128)S(1)}, pred[]{:T(512)}, ...), condition=%wide.region_7.8_spmd.clone, body=%wide.region_4.7_spmd.clone.sunk | while | flops 3149311 | bytes 1098969 | solution.py:78
  122.6 3.3 collective-permute-start.1
  126.5 2.5 collective-permute-start
  129.0 3.8 collective-permute-done
  136.1 3.9 collective-permute-start
  140.0 2.4 collective-permute-done
  145.7 3.9 collective-permute-start
  149.7 2.4 collective-permute-done
  155.3 3.9 collective-permute-start
  159.3 2.4 collective-permute-done
  164.9 3.9 collective-permute-start
  174.6 3.9 collective-permute-start
  184.2 3.9 collective-permute-start
  190.6 35.4 %while.56 = (s32[]{:T(128)}, f32[2,256]{1,0:T(2,128)S(1)}, f32[64,2,256]{2,0,1:T(8,128)S(1)}, f32[64,2]{1,0:T(8,128)S(1)}, pred[64,2]{1,0:T(8,128)(4,1)S(1)}, /*...) while((s32[]{:T(128)}, f32[2,256]{1,0:T(2,128)S(1)}, ...), condition=%wide.region_10.11_spmd, body=%wide.region_8.10_spmd.sunk | while | flops 1574914 | bytes 282793 | solution.py:89
  226.0 37.9 %while.57 = (s32[]{:T(128)}, f32[2,256]{1,0:T(2,128)S(1)}, f32[64,2,256]{2,0,1:T(8,128)S(1)}, pred[64,2]{1,0:T(8,128)(4,1)S(1)}, f32[64,2,256]{2,1,0:T(2,128)S(1...) while((s32[]{:T(128)}, f32[2,256]{1,0:T(2,128)S(1)}, f32[64,2,256]{2,0,1:T(8,128)S(1)}, ...), condition=%wide.region_13.14_spmd, body=%wide.region_11.13_spmd.sunk | while | flops 1574913 | bytes 282763 | solution.py:97
  264.3 3.4 scatter_custom_fusion
  267.7 20.5 %psum.15 = f32[2]{0:T(128)S(1)} all-reduce(f32[2]{0:T(128)S(1)} %reduce_sum.94), channel_id=1, replica_groups=mesh['tm'=8,'emit'=4] {'tm'}, use_global_device_ids=true, to_apply=%region_20.21 | all-reduce | flops 2 | bytes 16 | tf_op jit(solution)/shard_map/psum | solution.py:118
  289.4 100.2 %reduce-scatter.2.cloned.1.call-done = f32[128,256]{1,0:T(8,128)} async-done(((f32[4096,256]{1,0:T(8,128)}), f32[128,256]{1,0:T(8,128)}) %reduce-scatter.2.cloned.1.call-update) | async-done | bytes 131088 | tf_op jit(solution)/shard_map/reduce_scatter | solution.py:107
  390.6 63.3 %psum.14 = f32[256]{0:T(256)S(1)} all-reduce(f32[256]{0:T(256)S(1)} %reduce_sum.93), channel_id=1, replica_groups=mesh['tm'=8,'emit'=4] {'tm','emit'}, use_global_device_ids=true, to_apply=%region_18.19 | all-reduce | flops 256 | bytes 2048 | tf_op jit(solution)/shard_map/psum | solution.py:117
  (1141 shorter events, 156.1 us)
Async XLA Ops:
  10.7 5.5 %copy-start.1 = (s32[2,64]{1,0:T(2,128)S(1)}, s32[2,64]{1,0:T(2,128)}, u32[]{:S(2)}) copy-start(s32[2,64]{1,0:T(2,128)} %param.13) | copy-start | bytes 1540
  10.7 5.6 %copy-start.3 = (s32[2]{0:T(128)S(1)}, s32[2]{0:T(128)}, u32[]{:S(2)}) copy-start(s32[2]{0:T(128)} %param.14) | copy-start | bytes 28
  10.7 6.0 %copy-start.2 = (f32[256]{0:T(256)S(1)}, f32[256]{0:T(256)}, u32[]{:S(2)}) copy-start(f32[256]{0:T(256)} %param.15) | copy-start | bytes 3076
  10.7 55.3 %copy-start = (f32[256,256]{1,0:T(8,128)S(1)}, f32[256,256]{1,0:T(8,128)}, u32[]{:S(2)}) copy-start(f32[256,256]{1,0:T(8,128)} %param.16) | copy-start | bytes 786436
  10.7 52.1 %all-to-all-start = ((f32[4,1024,256]{2,1,0:T(8,128)}), f32[4,1024,256]{2,1,0:T(8,128)}, u32[]{:S(2)}, u32[]{:S(2)}) async-start(f32[4,1024,256]{2,1,0:T(8,128)} %tile.2), calls=%async_computation | async-start | bytes 8388608 | tf_op jit(solution)/shard_map/all_to_all | solution.py:13
  16.2 373.5 %reduce-scatter.2.cloned.1.call-start = ((), (), s32[]{:S(2)}) async-start(), calls=%async_computation.2 | async-start | bytes 4325376 | tf_op jit(solution)/shard_map/reduce_scatter | solution.py:107
  122.6 6.4 %collective-permute-start.1 = (f32[2,256]{1,0:T(2,128)S(1)}, f32[2,256]{1,0:T(2,128)S(1)}, u32[]{:S(2)}, u32[]{:S(2)}) collective-permute-start(f32[2,256]{1,0:T(2,128)S(1)} %bitcast_divide_fusion.5), channel_id=1, source_target_pairs={{4,0},{8,4},{12,8},{16,12},{20,16},{24,20},{28,24},{5,1},{9,5},{13... | collective-permute-start | bytes 6152 | tf_op jit(solution)/shard_map/while/body/eval_jaxpr/ppermute | solution.py:21
  126.5 6.4 %collective-permute-start = (f32[2,256]{1,0:T(2,128)S(1)}, f32[2,256]{1,0:T(2,128)S(1)}, u32[]{:S(2)}, u32[]{:S(2)}) collective-permute-start(f32[2,256]{1,0:T(2,128)S(1)} %bitcast_divide_fusion.4), channel_id=1, source_target_pairs={{0,4},{4,8},{8,12},{12,16},{16,20},{20,24},{24,28},{1,5},{5,9},{9,... | collective-permute-start | bytes 6152 | tf_op jit(solution)/shard_map/while/body/eval_jaxpr/ppermute | solution.py:21
  133.6 6.4 %collective-permute-start.1 = (f32[2,256]{1,0:T(2,128)S(1)}, f32[2,256]{1,0:T(2,128)S(1)}, u32[]{:S(2)}, u32[]{:S(2)}) collective-permute-start(f32[2,256]{1,0:T(2,128)S(1)} %bitcast_divide_fusion.5), channel_id=1, source_target_pairs={{4,0},{8,4},{12,8},{16,12},{20,16},{24,20},{28,24},{5,1},{9,5},{13... | collective-permute-start | bytes 6152 | tf_op jit(solution)/shard_map/while/body/eval_jaxpr/ppermute | solution.py:21
  136.1 6.4 %collective-permute-start = (f32[2,256]{1,0:T(2,128)S(1)}, f32[2,256]{1,0:T(2,128)S(1)}, u32[]{:S(2)}, u32[]{:S(2)}) collective-permute-start(f32[2,256]{1,0:T(2,128)S(1)} %bitcast_divide_fusion.4), channel_id=1, source_target_pairs={{0,4},{4,8},{8,12},{12,16},{16,20},{20,24},{24,28},{1,5},{5,9},{9,... | collective-permute-start | bytes 6152 | tf_op jit(solution)/shard_map/while/body/eval_jaxpr/ppermute | solution.py:21
  143.2 6.4 %collective-permute-start.1 = (f32[2,256]{1,0:T(2,128)S(1)}, f32[2,256]{1,0:T(2,128)S(1)}, u32[]{:S(2)}, u32[]{:S(2)}) collective-permute-start(f32[2,256]{1,0:T(2,128)S(1)} %bitcast_divide_fusion.5), channel_id=1, source_target_pairs={{4,0},{8,4},{12,8},{16,12},{20,16},{24,20},{28,24},{5,1},{9,5},{13... | collective-permute-start | bytes 6152 | tf_op jit(solution)/shard_map/while/body/eval_jaxpr/ppermute | solution.py:21
  145.7 6.4 %collective-permute-start = (f32[2,256]{1,0:T(2,128)S(1)}, f32[2,256]{1,0:T(2,128)S(1)}, u32[]{:S(2)}, u32[]{:S(2)}) collective-permute-start(f32[2,256]{1,0:T(2,128)S(1)} %bitcast_divide_fusion.4), channel_id=1, source_target_pairs={{0,4},{4,8},{8,12},{12,16},{16,20},{20,24},{24,28},{1,5},{5,9},{9,... | collective-permute-start | bytes 6152 | tf_op jit(solution)/shard_map/while/body/eval_jaxpr/ppermute | solution.py:21
  152.8 6.4 %collective-permute-start.1 = (f32[2,256]{1,0:T(2,128)S(1)}, f32[2,256]{1,0:T(2,128)S(1)}, u32[]{:S(2)}, u32[]{:S(2)}) collective-permute-start(f32[2,256]{1,0:T(2,128)S(1)} %bitcast_divide_fusion.5), channel_id=1, source_target_pairs={{4,0},{8,4},{12,8},{16,12},{20,16},{24,20},{28,24},{5,1},{9,5},{13... | collective-permute-start | bytes 6152 | tf_op jit(solution)/shard_map/while/body/eval_jaxpr/ppermute | solution.py:21
  155.3 6.4 %collective-permute-start = (f32[2,256]{1,0:T(2,128)S(1)}, f32[2,256]{1,0:T(2,128)S(1)}, u32[]{:S(2)}, u32[]{:S(2)}) collective-permute-start(f32[2,256]{1,0:T(2,128)S(1)} %bitcast_divide_fusion.4), channel_id=1, source_target_pairs={{0,4},{4,8},{8,12},{12,16},{16,20},{20,24},{24,28},{1,5},{5,9},{9,... | collective-permute-start | bytes 6152 | tf_op jit(solution)/shard_map/while/body/eval_jaxpr/ppermute | solution.py:21
  162.5 6.4 %collective-permute-start.1 = (f32[2,256]{1,0:T(2,128)S(1)}, f32[2,256]{1,0:T(2,128)S(1)}, u32[]{:S(2)}, u32[]{:S(2)}) collective-permute-start(f32[2,256]{1,0:T(2,128)S(1)} %bitcast_divide_fusion.5), channel_id=1, source_target_pairs={{4,0},{8,4},{12,8},{16,12},{20,16},{24,20},{28,24},{5,1},{9,5},{13... | collective-permute-start | bytes 6152 | tf_op jit(solution)/shard_map/while/body/eval_jaxpr/ppermute | solution.py:21
  164.9 6.4 %collective-permute-start = (f32[2,256]{1,0:T(2,128)S(1)}, f32[2,256]{1,0:T(2,128)S(1)}, u32[]{:S(2)}, u32[]{:S(2)}) collective-permute-start(f32[2,256]{1,0:T(2,128)S(1)} %bitcast_divide_fusion.4), channel_id=1, source_target_pairs={{0,4},{4,8},{8,12},{12,16},{16,20},{20,24},{24,28},{1,5},{5,9},{9,... | collective-permute-start | bytes 6152 | tf_op jit(solution)/shard_map/while/body/eval_jaxpr/ppermute | solution.py:21
  172.1 6.4 %collective-permute-start.1 = (f32[2,256]{1,0:T(2,128)S(1)}, f32[2,256]{1,0:T(2,128)S(1)}, u32[]{:S(2)}, u32[]{:S(2)}) collective-permute-start(f32[2,256]{1,0:T(2,128)S(1)} %bitcast_divide_fusion.5), channel_id=1, source_target_pairs={{4,0},{8,4},{12,8},{16,12},{20,16},{24,20},{28,24},{5,1},{9,5},{13... | collective-permute-start | bytes 6152 | tf_op jit(solution)/shard_map/while/body/eval_jaxpr/ppermute | solution.py:21
  174.6 6.4 %collective-permute-start = (f32[2,256]{1,0:T(2,128)S(1)}, f32[2,256]{1,0:T(2,128)S(1)}, u32[]{:S(2)}, u32[]{:S(2)}) collective-permute-start(f32[2,256]{1,0:T(2,128)S(1)} %bitcast_divide_fusion.4), channel_id=1, source_target_pairs={{0,4},{4,8},{8,12},{12,16},{16,20},{20,24},{24,28},{1,5},{5,9},{9,... | collective-permute-start | bytes 6152 | tf_op jit(solution)/shard_map/while/body/eval_jaxpr/ppermute | solution.py:21
  181.7 6.4 %collective-permute-start.1 = (f32[2,256]{1,0:T(2,128)S(1)}, f32[2,256]{1,0:T(2,128)S(1)}, u32[]{:S(2)}, u32[]{:S(2)}) collective-permute-start(f32[2,256]{1,0:T(2,128)S(1)} %bitcast_divide_fusion.5), channel_id=1, source_target_pairs={{4,0},{8,4},{12,8},{16,12},{20,16},{24,20},{28,24},{5,1},{9,5},{13... | collective-permute-start | bytes 6152 | tf_op jit(solution)/shard_map/while/body/eval_jaxpr/ppermute | solution.py:21
  184.2 6.4 %collective-permute-start = (f32[2,256]{1,0:T(2,128)S(1)}, f32[2,256]{1,0:T(2,128)S(1)}, u32[]{:S(2)}, u32[]{:S(2)}) collective-permute-start(f32[2,256]{1,0:T(2,128)S(1)} %bitcast_divide_fusion.4), channel_id=1, source_target_pairs={{0,4},{4,8},{8,12},{12,16},{16,20},{20,24},{24,28},{1,5},{5,9},{9,... | collective-permute-start | bytes 6152 | tf_op jit(solution)/shard_map/while/body/eval_jaxpr/ppermute | solution.py:21
Sparse Core Ops, SparseCore 0:
  267.8 121.7 reduce-scatter.1
